TPU v7x, 256 devices: a whole 4x4x8 slice. The times are simulated.
256 devices in a mesh: dp: 32 (over y, x, core), tensor: 8 (over z).
Axes of the slice: x: 4, y: 4, z: 8, core: 2. Of those that a mesh axis runs over, the one named last changes fastest.
Arguments:
- patches: bfloat16 [16384, 1280], P('dp'), may hold values from -6 to 6
- window_ids: int32 [32, 512], P('dp'), may hold values from 0 to 15, never falling along the last dimension, each value on 1 to 64 neighbouring positions
- vit_gain: float32 [1280], replicated, may hold values from 0.5 to 2
- qkv_weight: bfloat16 [3, 1280, 1280], P(None, None, 'tensor'), may hold values from -0.15625 to 0.15625
- out_weight: bfloat16 [1280, 1280], P('tensor'), may hold values from -0.15625 to 0.15625
- merge_gain: float32 [1280], replicated, may hold values from 0.5 to 2
- merger_weight: bfloat16 [5120, 3584], P(None, 'tensor'), may hold values from -0.078125 to 0.078125
- audio: bfloat16 [12288, 3584], P('dp', 'tensor'), may hold values from -6 to 6
- span_lengths: int32 [32, 32], replicated, may hold values from 8 to 32, as said below
- span_time: int32 [32, 32], replicated, may hold values from 0 to 31, each once within a row
- llm_gain: float32 [3584], replicated, may hold values from 0.5 to 2
- gate_weight: bfloat16 [3584, 9472], P('dp', 'tensor'), may hold values from -0.09375 to 0.09375
- up_weight: bfloat16 [3584, 9472], P('dp', 'tensor'), may hold values from -0.09375 to 0.09375
- down_weight: bfloat16 [9472, 3584], P('tensor', 'dp'), may hold values from -0.0625 to 0.0625
Outputs:
- mixed: bfloat16 [16384, 3584], P(('dp', 'tensor'))
Inputs may be any that keep to these rules, and one draw needn't show every extreme that they name: `span_lengths`: every row and every column sums to 512; every row and every column holds the value 32 at least once. `span_time`: each row is a permutation of the owners' numbers. `window_ids`: window numbers never fall along a row; a window holds at most 64 patches.
All inputs are finite; a program needn't handle non-finite values.
Results may differ from a plain program's by a relative error of at most 0.017.
Values may be sent and summed in bfloat16 or wider, within the bound.
No kernel may reach another device: no remote copies, remote signals or barrier semaphores. Data moves between devices by JAX's collectives and lax.ppermute only.
A program may use at most 128 MiB of HBM per device.

v0:
```python
import math
import jax
import jax.numpy as jnp
from jax import lax
from jax.sharding import PartitionSpec as P

D_VIT = 1280
HEAD_VIT = 80
EPSILON = 1e-06


def in_blocks(x, dim, devices):
    before, after = (x.shape[:dim], x.shape[dim + 1 :])
    return jnp.moveaxis(x.reshape(*before, devices, -1, *after), dim, 0)


def sent_and_summed(x, axis, dim):
    parts = in_blocks(x, dim, lax.axis_size(axis))
    arrived = lax.all_to_all(parts, axis, split_axis=0, concat_axis=0, tiled=True)
    return arrived.astype(jnp.float32).sum(axis=0)


def from_everyone(x, axis):
    devices = lax.axis_size(axis)
    return lax.all_to_all(jnp.broadcast_to(x[None], (devices, *x.shape)), axis, 0, 0, tiled=True)


def in_order(parts, dim):
    parts = jnp.moveaxis(parts, 0, dim)
    dims = parts.shape
    return parts.reshape(*dims[:dim], dims[dim] * dims[dim + 1], *dims[dim + 2 :])


def gather_directly(x, axis, dim):
    parts = from_everyone(x, axis)
    return in_order(parts, dim)


def gather_turned(arrays, axis, dims):
    turned = [jnp.moveaxis(a, dim, 0) for a, dim in zip(arrays, dims)]
    widths = [t[0].size for t in turned]
    both = jnp.concatenate([t.reshape(-1, w) for t, w in zip(turned, widths)], axis=1)
    whole = lax.all_gather(both, axis, axis=0, tiled=True)
    parts = jnp.split(whole, [sum(widths[:k]) for k in range(1, len(widths))], axis=1)
    return tuple(
        (
            jnp.moveaxis(b.reshape(-1, *t.shape[1:]), 0, dim)
            for b, t, dim in zip(parts, turned, dims)
        )
    )


def rms_scale(values, gain):
    wide = values.astype(jnp.float32)
    meansq = jnp.mean(wide * wide, axis=-1, keepdims=True)
    return wide * lax.rsqrt(meansq + EPSILON) * gain


def body(
    patches,
    window_ids,
    vit_gain,
    qkv_weight,
    out_weight,
    merge_gain,
    merger_weight,
    audio,
    span_lengths,
    span_time,
    llm_gain,
    gate_weight,
    up_weight,
    down_weight,
):
    patch_count = patches.shape[0]
    heads_here = qkv_weight.shape[2] // HEAD_VIT
    normed = rms_scale(patches, vit_gain).astype(jnp.bfloat16)
    query = jnp.dot(normed, qkv_weight[0], preferred_element_type=jnp.float32).astype(jnp.bfloat16)
    keys = jnp.dot(normed, qkv_weight[1], preferred_element_type=jnp.float32).astype(jnp.bfloat16)
    values = jnp.dot(normed, qkv_weight[2], preferred_element_type=jnp.float32).astype(jnp.bfloat16)
    query = query.reshape(patch_count, heads_here, HEAD_VIT)
    keys = keys.reshape(patch_count, heads_here, HEAD_VIT)
    values = values.reshape(patch_count, heads_here, HEAD_VIT)
    scores = jnp.einsum(
        "phe,qhe->hpq", query, keys, preferred_element_type=jnp.float32
    ) / math.sqrt(HEAD_VIT)
    windows = window_ids[0]
    same = windows[:, None] == windows[None, :]
    scores = jnp.where(same[None], scores, -1e30)
    probs = jax.nn.softmax(scores, axis=-1).astype(jnp.bfloat16)
    context = jnp.einsum("hpq,qhe->phe", probs, values, preferred_element_type=jnp.float32).astype(
        jnp.bfloat16
    )
    context = context.reshape(patch_count, heads_here * HEAD_VIT)
    partial_value = jnp.dot(context, out_weight, preferred_element_type=jnp.float32)
    share = sent_and_summed(partial_value.astype(jnp.bfloat16), "tensor", 0)
    share_rows = share.shape[0]
    own_frames = lax.dynamic_slice_in_dim(
        patches, lax.axis_index("tensor") * share_rows, share_rows, 0
    )
    own_encoded = (own_frames.astype(jnp.float32) + share).astype(jnp.bfloat16)
    encoded = gather_directly(own_encoded, "tensor", 0)
    merged = (
        rms_scale(encoded, merge_gain).astype(jnp.bfloat16).reshape(patch_count // 4, 4 * D_VIT)
    )
    video = jnp.dot(merged, merger_weight, preferred_element_type=jnp.float32).astype(jnp.bfloat16)
    source = jnp.concatenate([video, audio], axis=0)
    seq_count = source.shape[0]
    owner_count = lax.axis_size("dp")
    owner = lax.axis_index("dp")
    capacity = 2 * seq_count // owner_count
    sent_lengths = span_lengths[owner]
    starts = jnp.cumsum(sent_lengths) - sent_lengths
    slot_index = jnp.arange(capacity, dtype=jnp.int32)
    occupied = slot_index[None, :] < sent_lengths[:, None]
    source_index = jnp.where(occupied, starts[:, None] + slot_index[None, :], 0).reshape(-1)
    outgoing = jnp.take(source, source_index, axis=0)
    outgoing = jnp.where(occupied.reshape(-1)[:, None], outgoing, jnp.zeros((), outgoing.dtype))
    incoming = lax.all_to_all(outgoing, "dp", split_axis=0, concat_axis=0, tiled=True)
    taken_lengths = span_lengths[:, owner]
    arrival = span_time[owner]
    earlier = arrival[:, None] < arrival[None, :]
    offsets = jnp.sum(jnp.where(earlier, taken_lengths[:, None], 0), axis=0)
    position = jnp.arange(seq_count, dtype=jnp.int32)
    inside = (position[None, :] >= offsets[:, None]) & (
        position[None, :] < offsets[:, None] + taken_lengths[:, None]
    )
    sender = jnp.arange(owner_count, dtype=jnp.int32)[:, None]
    slot_row = sender * capacity + position[None, :] - offsets[:, None]
    picked = jnp.sum(jnp.where(inside, slot_row, 0), axis=0)
    sequence = jnp.take(incoming, picked, axis=0)
    features = lax.all_gather(sequence, "tensor", axis=1, tiled=True)
    normed_seq = rms_scale(features, llm_gain).astype(jnp.bfloat16)
    gate_full, up_full, down_full = gather_turned(
        (gate_weight, up_weight, down_weight), "dp", (0, 0, 1)
    )
    gate = jnp.dot(normed_seq, gate_full, preferred_element_type=jnp.float32)
    upward = jnp.dot(normed_seq, up_full, preferred_element_type=jnp.float32)
    hidden = (jax.nn.silu(gate) * upward).astype(jnp.bfloat16)
    terms = jnp.dot(hidden, down_full, preferred_element_type=jnp.float32)
    summed = lax.psum_scatter(
        terms.astype(jnp.bfloat16), "tensor", scatter_dimension=0, tiled=True
    ).astype(jnp.float32)
    own_count = summed.shape[0]
    own_rows = lax.dynamic_slice_in_dim(
        features, lax.axis_index("tensor") * own_count, own_count, 0
    )
    return (own_rows.astype(jnp.float32) + summed).astype(jnp.bfloat16)


def solution(mesh):
    return jax.shard_map(
        body,
        mesh=mesh,
        in_specs=(
            P("dp", None),
            P("dp", None),
            P(),
            P(None, None, "tensor"),
            P("tensor", None),
            P(),
            P(None, "tensor"),
            P("dp", "tensor"),
            P(),
            P(),
            P(),
            P("dp", "tensor"),
            P("dp", "tensor"),
            P("tensor", "dp"),
        ),
        out_specs=P(("dp", "tensor"), None),
        check_vma=False,
    )
```

profile of v0, /device:TPU:1, one launch (start us, length us, event | category | flops | bytes accessed | tf_op | source)
XLA Modules:
  0.0 377.8 jit_solution(1047735685525039576)
XLA Ops:
  6.5 1.8 fusion.19
  8.4 2.1 convolution_convert_fusion.3
  14.3 1.6 convolution_convert_fusion
  15.9 9.0 %all-to-all-start = ((bf16[8,64,1280]{2,1,0:T(8,128)(2,1)}), bf16[8,64,1280]{2,1,0:T(8,128)(2,1)S(1)}, u32[]{:S(2)}, u32[]{:S(2)}) async-start(bf16[8,64,1280]{2,1,0:T(8,128)(2,1)} %bitcast.15), calls=%async_computation | async-start | bytes 2621440 | tf_op jit(solution)/shard_map/all_to_all | solution.py:19
  24.9 34.9 %all-to-all-done = bf16[8,64,1280]{2,1,0:T(8,128)(2,1)S(1)} async-done(((bf16[8,64,1280]{2,1,0:T(8,128)(2,1)}), bf16[8,64,1280]{2,1,0:T(8,128)(2,1)S(1)}, u32[]{:S(2)}, u32[]{:S(2)}) %all-to-all-start) | async-done | bytes 1310752 | tf_op jit(solution)/shard_map/all_to_all | solution.py:19
  61.2 3.6 all-to-all-start.1
  66.6 32.9 %all-to-all-done.1 = bf16[8,64,1280]{2,1,0:T(8,128)(2,1)S(1)} async-done(((bf16[8,64,1280]{2,1,0:T(8,128)(2,1)}), bf16[8,64,1280]{2,1,0:T(8,128)(2,1)S(1)}, u32[]{:S(2)}, u32[]{:S(2)}) %all-to-all-start.1) | async-done | bytes 1310752 | tf_op jit(solution)/shard_map/all_to_all | solution.py:25
  100.4 2.0 copy.42
  102.3 1.9 reshape.242
  104.2 5.2 %fusion.25 = bf16[128,448]{0,1:T(8,128)(2,1)S(1)} fusion(bf16[5120,448]{0,1:T(8,128)(2,1)} %param.20, f32[128,5120]{1,0:T(8,128)} %reshape.242, f32[128,5120]{1,0:T(8,128)} %bitcast.49, f32[5120]{0:T(1024)S(1)} %mul.101), kind=kOutput, calls=%fused_computation.36 | convolution fusion | flops 589225984 | bytes 9965568 | tf_op jit(solution)/shard_map/dot_general | solution.py:106
  109.6 4.0 %gather_fusion = bf16[1024,448]{1,0:T(8,128)(2,1)S(1)} fusion(bf16[512,448]{1,0:T(8,128)(2,1)S(1)} %pad_maximum_fusion, s32[1024]{0:T(1024)S(1)} %broadcast_clamp_fusion), kind=kCustom, calls=%fused_computation | custom fusion | bytes 1839104 | tf_op jit(solution)/shard_map/jit(_take)/gather | solution.py:117
  113.6 1.3 select_select_fusion
  114.9 7.6 %all-to-all-start.2 = ((bf16[32,32,448]{2,1,0:T(8,128)(2,1)}), bf16[32,32,448]{2,1,0:T(8,128)(2,1)S(1)}, u32[]{:S(2)}, u32[]{:S(2)}) async-start(bf16[32,32,448]{2,1,0:T(8,128)(2,1)} %select_select_fusion), calls=%async_computation.2 | async-start | bytes 2097152 | tf_op jit(solution)/shard_map/all_to_all | solution.py:119
  122.6 17.0 %all-to-all-done.2 = bf16[32,32,448]{2,1,0:T(8,128)(2,1)S(1)} async-done(((bf16[32,32,448]{2,1,0:T(8,128)(2,1)}), bf16[32,32,448]{2,1,0:T(8,128)(2,1)S(1)}, u32[]{:S(2)}, u32[]{:S(2)}) %all-to-all-start.2) | async-done | bytes 917536 | tf_op jit(solution)/shard_map/all_to_all | solution.py:119
  139.6 2.0 gather_fusion.1
  142.8 1.4 concatenate.7
  144.4 40.7 %all-gather.3.cloned.1.call-done = bf16[512,3584]{0,1:T(8,128)(2,1)} async-done(((bf16[512,448]{0,1:T(8,128)(2,1)}), bf16[512,3584]{0,1:T(8,128)(2,1)}) %all-gather.3.cloned.1.call-update) | async-done | bytes 3670032 | tf_op jit(solution)/shard_map/all_gather | solution.py:132
  185.1 2.9 fusion.7
  188.0 97.1 %all-gather.5.cloned.1.call-done = bf16[3584,3552]{1,0:T(8,128)(2,1)} async-done(((bf16[112,3552]{1,0:T(8,128)(2,1)}), bf16[3584,3552]{1,0:T(8,128)(2,1)}) %all-gather.5.cloned.1.call-update) | async-done | bytes 25460752 | tf_op jit(solution)/shard_map/all_gather | solution.py:43
  285.1 9.8 %fusion.5 = f32[512,1184]{0,1:T(8,128)S(1)} fusion(bf16[3584,3552]{1,0:T(8,128)(2,1)} %all-gather.5.cloned.1.call-done, bf16[512,3584]{0,1:T(8,128)(2,1)} %all-gather.3.cloned.1.call-done, f32[3584]{0:T(1024)S(1)} %copy-done.11, f32[512]{0:T(512)S(1)} %add_rsqrt_fusion.1), kind=kOutput, calls=%fused_computation.7 | convolution fusion | flops 4352638976 | bytes 15286272 | tf_op jit(solution)/shard_map/dot_general | solution.py:137
  294.9 24.9 %fusion.10 = bf16[512,3584]{1,0:T(8,128)(2,1)} fusion(bf16[3584,3552]{1,0:T(8,128)(2,1)} %all-gather.5.cloned.1.call-done, f32[512,1184]{0,1:T(8,128)S(1)} %fusion.5, bf16[512,3584]{0,1:T(8,128)(2,1)} %all-gather.3.cloned.1.call-done, f32[3584]{0:T(1024)S(1)} %copy-done.11, f32[512]{0:T(512)S(1)} %add_rsqrt_fusion.1), kind=kOutput, calls=%fused_computation.14 | convolution fusion | flops 8703410176 | bytes 28131328 | tf_op jit(solution)/shard_map/dot_general | solution.py:140
  319.8 1.6 constant_dynamic-slice_fusion
  321.7 47.7 %reduce-scatter.2.cloned.1.call-done = bf16[64,3584]{1,0:T(8,128)(2,1)} async-done(((bf16[512,3584]{1,0:T(8,128)(2,1)}), bf16[64,3584]{1,0:T(8,128)(2,1)}) %reduce-scatter.2.cloned.1.call-update) | async-done | bytes 458768 | tf_op jit(solution)/shard_map/reduce_scatter | solution.py:141
  369.4 1.9 add_convert_fusion
  (74 shorter events, 9.8 us)
Async XLA Ops:
  6.5 7.7 %copy-start = (bf16[160,1280]{1,0:T(8,128)(2,1)S(1)}, bf16[160,1280]{1,0:T(8,128)(2,1)}, u32[]{:S(2)}) copy-start(bf16[160,1280]{1,0:T(8,128)(2,1)} %param.18) | copy-start | bytes 1228804
  6.5 3.9 %copy-start.2 = (bf16[512,1280]{1,0:T(8,128)(2,1)S(1)}, bf16[512,1280]{1,0:T(8,128)(2,1)}, u32[]{:S(2)}) copy-start(bf16[512,1280]{1,0:T(8,128)(2,1)} %param.14) | copy-start | bytes 3932164
  6.5 3.9 %copy-start.12 = (f32[1280]{0:T(1024)S(1)}, f32[1280]{0:T(1024)}, u32[]{:S(2)}) copy-start(f32[1280]{0:T(1024)} %param.16) | copy-start | bytes 15364
  6.5 3.9 %copy-start.10 = (bf16[3,1280,160]{1,2,0:T(8,128)(2,1)S(1)}, bf16[3,1280,160]{1,2,0:T(8,128)(2,1)}, u32[]{:S(2)}) copy-start(bf16[3,1280,160]{1,2,0:T(8,128)(2,1)} %param.17) | copy-start | bytes 3686404
  10.5 1.3 copy-start.8
  15.9 43.9 %all-to-all-start = ((bf16[8,64,1280]{2,1,0:T(8,128)(2,1)}), bf16[8,64,1280]{2,1,0:T(8,128)(2,1)S(1)}, u32[]{:S(2)}, u32[]{:S(2)}) async-start(bf16[8,64,1280]{2,1,0:T(8,128)(2,1)} %bitcast.15), calls=%async_computation | async-start | bytes 2621440 | tf_op jit(solution)/shard_map/all_to_all | solution.py:19
  60.0 4.8 %copy-start.9 = (f32[1280]{0:T(1024)S(1)}, f32[1280]{0:T(1024)}, u32[]{:S(2)}) copy-start(f32[1280]{0:T(1024)} %param.19) | copy-start | bytes 15364
  60.0 4.8 %copy-start.3 = (bf16[384,448]{0,1:T(8,128)(2,1)S(1)}, bf16[384,448]{0,1:T(8,128)(2,1)}, u32[]{:S(2)}) copy-start(bf16[384,448]{0,1:T(8,128)(2,1)} %param.21) | copy-start | bytes 1032196
  60.0 5.0 %copy-start.7 = (s32[32,32]{1,0:T(8,128)S(1)}, s32[32,32]{1,0:T(8,128)}, u32[]{:S(2)}) copy-start(s32[32,32]{1,0:T(8,128)} %param.22) | copy-start | bytes 12292
  61.2 38.3 %all-to-all-start.1 = ((bf16[8,64,1280]{2,1,0:T(8,128)(2,1)}), bf16[8,64,1280]{2,1,0:T(8,128)(2,1)S(1)}, u32[]{:S(2)}, u32[]{:S(2)}) async-start(bf16[8,64,1280]{2,1,0:T(8,128)(2,1)} %broadcast_in_dim.103), calls=%async_computation.1 | async-start | bytes 2621440 | tf_op jit(solution)/shard_map/all_to_all | solution.py:25
  114.9 24.8 %all-to-all-start.2 = ((bf16[32,32,448]{2,1,0:T(8,128)(2,1)}), bf16[32,32,448]{2,1,0:T(8,128)(2,1)S(1)}, u32[]{:S(2)}, u32[]{:S(2)}) async-start(bf16[32,32,448]{2,1,0:T(8,128)(2,1)} %select_select_fusion), calls=%async_computation.2 | async-start | bytes 2097152 | tf_op jit(solution)/shard_map/all_to_all | solution.py:119
  122.4 62.7 %all-gather.3.cloned.1.call-start = ((), (), s32[]{:S(2)}) async-start(), calls=%async_computation.4 | async-start | bytes 4128768 | tf_op jit(solution)/shard_map/all_gather | solution.py:132
  139.6 3.2 copy-start.4
  139.6 3.2 copy-start.5
  139.6 3.2 copy-start.6
  142.7 142.4 %all-gather.5.cloned.1.call-start = ((), (), s32[]{:S(2)}) async-start(), calls=%async_computation.5 | async-start | bytes 26492928 | tf_op jit(solution)/shard_map/all_gather | solution.py:43
  144.1 141.0 %copy-start.11 = (f32[3584]{0:T(1024)S(1)}, f32[3584]{0:T(1024)}, u32[]{:S(2)}) copy-start(f32[3584]{0:T(1024)} %param.24) | copy-start | bytes 43012
  144.2 225.2 %reduce-scatter.2.cloned.1.call-start = ((), (), s32[]{:S(2)}) async-start(), calls=%async_computation.6 | async-start | bytes 4128768 | tf_op jit(solution)/shard_map/reduce_scatter | solution.py:141
  319.8 51.5 %copy-start.1 = (bf16[160,1280]{1,0:T(8,128)(2,1)S(1)}, bf16[160,1280]{1,0:T(8,128)(2,1)}, u32[]{:S(2)}) copy-start(bf16[160,1280]{1,0:T(8,128)(2,1)} %param.18) | copy-start | bytes 1228804
Sparse Core Ops, SparseCore 0:
  142.8 42.2 all-gather.2
  187.7 97.3 all-gather.4
  319.9 49.4 reduce-scatter.1
where the time goes:
time: 378 us
  waiting for transfers between devices  270 us (71%)
  matrix products  47.1 us (12%)
  starting transfers between devices  20.5 us (5%)
  local copies, waits for them, and re-layouts  17 us (4%)
  between operations  13.5 us (4%)
  other arithmetic  9.35 us (2%)
    all_gather x1, waiting for transfers between devices, gather_turned(): whole = lax.all_gather(both, axis, axis=0, tiled=True)  97.1 us
    reduce_scatter x1, waiting for transfers between devices, body(): lax.psum_scatter(terms.astype(jnp.bfloat16), 'tensor', scatter_dimension=...  47.7 us
    all_gather x1, waiting for transfers between devices, body(): features = lax.all_gather(sequence, 'tensor', axis=1, tiled=True)  40.7 us
    all_to_all x1, waiting for transfers between devices, sent_and_summed(): lax.all_to_all(parts, axis, split_axis=0, concat_axis=0, tiled=True)  34.9 us
    all_to_all x1, waiting for transfers between devices, from_everyone(): lax.all_to_all(jnp.broadcast_to(x[None], (devices, *x.shape)), axis, 0, 0...  32.9 us
    dot_general x1, matrix products, body(): terms = jnp.dot(hidden, down_full, preferred_element_type=jnp.float32)  24.9 us
    all_to_all x1, waiting for transfers between devices, body(): lax.all_to_all(outgoing, 'dp', split_axis=0, concat_axis=0, tiled=True)  17 us
    dot_general x1, matrix products, body(): gate = jnp.dot(normed_seq, gate_full, preferred_element_type=jnp.float32)  9.77 us
  transfers between devices with their start and end apart: 6, of which 6 were waited for; matrix products, arithmetic and copies ran while one was open for 2% of the time, Pallas kernels for 0%

commit v1 on v0

--- a/solution.py
+++ b/solution.py
@@ -40,7 +40,10 @@
     turned = [jnp.moveaxis(a, dim, 0) for a, dim in zip(arrays, dims)]
     widths = [t[0].size for t in turned]
     both = jnp.concatenate([t.reshape(-1, w) for t, w in zip(turned, widths)], axis=1)
-    whole = lax.all_gather(both, axis, axis=0, tiled=True)
+    size = lax.axis_size(axis)
+    pieces = jnp.stack([both for _ in range(size)])
+    pieces = lax.all_to_all(pieces, axis, split_axis=0, concat_axis=0)
+    whole = jnp.concatenate(pieces, axis=0)
     parts = jnp.split(whole, [sum(widths[:k]) for k in range(1, len(widths))], axis=1)
     return tuple(
         (

time: 378 us -> 568 us (1.50)
  waiting for transfers between devices: 270 us -> 446 us
  local copies, waits for them, and re-layouts: 17 us -> 24.8 us
    all_to_all x0 -> x1, waiting for transfers between devices: none -> 257 us  [gather_turned(): pieces = lax.all_to_all(pieces, axis, split_axis=0, concat_axis=0)]
    all_gather x1 -> x0, waiting for transfers between devices: 97.1 us -> none  [gather_turned(): whole = lax.all_gather(both, axis, axis=0, tiled=True)]
    reduce_scatter x1, waiting for transfers between devices: 47.7 us -> 57.7 us  [body(): lax.psum_scatter(terms.astype(jnp.bfloat16), 'tensor', scatter_dimension=...]
    another operation x2 -> x3, local copies, waits for them, and re-layouts: 0.1 us -> 8.68 us  [the longest x1 8.58 us: gather_turned(): pieces = jnp.stack([both for _ in range(size)])]
where the time goes in v1:
time: 568 us; the launch traced here: 567 us
  waiting for transfers between devices  446 us (79%)
  matrix products  47 us (8%)
  starting transfers between devices  25.8 us (5%)
  local copies, waits for them, and re-layouts  24.8 us (4%)
  between operations  13.8 us (2%)
  other arithmetic  9.36 us (2%)
    all_to_all x1, waiting for transfers between devices, gather_turned(): pieces = lax.all_to_all(pieces, axis, split_axis=0, concat_axis=0)  257 us
    reduce_scatter x1, waiting for transfers between devices, body(): lax.psum_scatter(terms.astype(jnp.bfloat16), 'tensor', scatter_dimension=...  57.7 us
    all_gather x1, waiting for transfers between devices, body(): features = lax.all_gather(sequence, 'tensor', axis=1, tiled=True)  45.9 us
    all_to_all x1, waiting for transfers between devices, sent_and_summed(): lax.all_to_all(parts, axis, split_axis=0, concat_axis=0, tiled=True)  34.9 us
    all_to_all x1, waiting for transfers between devices, from_everyone(): lax.all_to_all(jnp.broadcast_to(x[None], (devices, *x.shape)), axis, 0, 0...  33.9 us
    dot_general x1, matrix products, body(): terms = jnp.dot(hidden, down_full, preferred_element_type=jnp.float32)  24.9 us
    all_to_all x1, waiting for transfers between devices, body(): lax.all_to_all(outgoing, 'dp', split_axis=0, concat_axis=0, tiled=True)  16.6 us
  transfers between devices with their start and end apart: 6, of which 6 were waited for; matrix products, arithmetic and copies ran while one was open for 2% of the time, Pallas kernels for 0%

profile of v1, /device:TPU:1, one launch (start us, length us, event | category | flops | bytes accessed | tf_op | source)
XLA Modules:
  0.0 567.2 jit_solution(12623454068268925336)
XLA Ops:
  6.5 1.8 fusion.19
  8.4 2.1 convolution_convert_fusion.4
  14.3 1.6 convolution_convert_fusion
  15.9 9.0 %all-to-all-start = ((bf16[8,64,1280]{2,1,0:T(8,128)(2,1)}), bf16[8,64,1280]{2,1,0:T(8,128)(2,1)S(1)}, u32[]{:S(2)}, u32[]{:S(2)}) async-start(bf16[8,64,1280]{2,1,0:T(8,128)(2,1)} %bitcast.15), calls=%async_computation | async-start | bytes 2621440 | tf_op jit(solution)/shard_map/all_to_all | solution.py:19
  24.9 34.9 %all-to-all-done = bf16[8,64,1280]{2,1,0:T(8,128)(2,1)S(1)} async-done(((bf16[8,64,1280]{2,1,0:T(8,128)(2,1)}), bf16[8,64,1280]{2,1,0:T(8,128)(2,1)S(1)}, u32[]{:S(2)}, u32[]{:S(2)}) %all-to-all-start) | async-done | bytes 1310752 | tf_op jit(solution)/shard_map/all_to_all | solution.py:19
  61.2 3.6 all-to-all-start.1
  65.6 33.9 %all-to-all-done.1 = bf16[8,64,1280]{2,1,0:T(8,128)(2,1)S(1)} async-done(((bf16[8,64,1280]{2,1,0:T(8,128)(2,1)}), bf16[8,64,1280]{2,1,0:T(8,128)(2,1)S(1)}, u32[]{:S(2)}, u32[]{:S(2)}) %all-to-all-start.1) | async-done | bytes 1310752 | tf_op jit(solution)/shard_map/all_to_all | solution.py:25
  100.4 2.0 copy.42
  102.3 1.9 reshape.248
  104.2 5.2 fusion.25
  109.6 4.0 gather_fusion
  114.9 7.6 %all-to-all-start.2 = ((bf16[32,32,448]{2,1,0:T(8,128)(2,1)}), bf16[32,32,448]{2,1,0:T(8,128)(2,1)S(1)}, u32[]{:S(2)}, u32[]{:S(2)}) async-start(bf16[32,32,448]{2,1,0:T(8,128)(2,1)} %select_select_fusion), calls=%async_computation.2 | async-start | bytes 2097152 | tf_op jit(solution)/shard_map/all_to_all | solution.py:122
  123.1 16.6 %all-to-all-done.2 = bf16[32,32,448]{2,1,0:T(8,128)(2,1)S(1)} async-done(((bf16[32,32,448]{2,1,0:T(8,128)(2,1)}), bf16[32,32,448]{2,1,0:T(8,128)(2,1)S(1)}, u32[]{:S(2)}, u32[]{:S(2)}) %all-to-all-start.2) | async-done | bytes 917536 | tf_op jit(solution)/shard_map/all_to_all | solution.py:122
  139.6 8.6 %stack.2 = bf16[32,112,3552]{2,1,0:T(8,128)(2,1)} broadcast(bf16[112,3552]{1,0:T(8,128)(2,1)S(1)} %concatenate.7), dimensions={1,2} | broadcast | bytes 26256384 | tf_op jit(solution)/shard_map/stack | solution.py:44
  148.2 5.3 all-to-all-start.3
  154.7 2.0 gather_fusion.1
  158.1 45.9 %all-gather.2.cloned.1.call-done = bf16[512,3584]{0,1:T(8,128)(2,1)} async-done(((bf16[512,448]{0,1:T(8,128)(2,1)}), bf16[512,3584]{0,1:T(8,128)(2,1)}) %all-gather.2.cloned.1.call-update) | async-done | bytes 3670032 | tf_op jit(solution)/shard_map/all_gather | solution.py:135
  204.0 2.9 fusion.7
  206.9 257.3 %all-to-all-done.3 = bf16[32,112,3552]{2,1,0:T(8,128)(2,1)} async-done(((bf16[32,112,3552]{2,1,0:T(8,128)(2,1)}), bf16[32,112,3552]{2,1,0:T(8,128)(2,1)}, u32[]{:S(2)}, u32[]{:S(2)}) %all-to-all-start.3) | async-done | bytes 25460768 | tf_op jit(solution)/shard_map/all_to_all | solution.py:45
  464.2 9.7 %fusion.5 = f32[512,1184]{0,1:T(8,128)S(1)} fusion(bf16[3584,3552]{1,0:T(8,128)(2,1)} %bitcast.22, bf16[512,3584]{0,1:T(8,128)(2,1)} %all-gather.2.cloned.1.call-done, f32[3584]{0:T(1024)S(1)} %copy-done.11, f32[512]{0:T(512)S(1)} %add_rsqrt_fusion.1), kind=kOutput, calls=%fused_computation.7 | convolution fusion | flops 4352638976 | bytes 15286272 | tf_op jit(solution)/shard_map/dot_general | solution.py:140
  473.9 24.9 %fusion.10 = bf16[512,3584]{1,0:T(8,128)(2,1)} fusion(bf16[3584,3552]{1,0:T(8,128)(2,1)} %bitcast.22, f32[512,1184]{0,1:T(8,128)S(1)} %fusion.5, bf16[512,3584]{0,1:T(8,128)(2,1)} %all-gather.2.cloned.1.call-done, f32[3584]{0:T(1024)S(1)} %copy-done.11, f32[512]{0:T(512)S(1)} %add_rsqrt_fusion.1), kind=kOutput, calls=%fused_computation.14 | convolution fusion | flops 8703410176 | bytes 28131328 | tf_op jit(solution)/shard_map/dot_general | solution.py:143
  498.8 1.6 constant_dynamic-slice_fusion
  500.7 57.7 %reduce-scatter.2.cloned.1.call-done = bf16[64,3584]{1,0:T(8,128)(2,1)} async-done(((bf16[512,3584]{1,0:T(8,128)(2,1)}), bf16[64,3584]{1,0:T(8,128)(2,1)}) %reduce-scatter.2.cloned.1.call-update) | async-done | bytes 458768 | tf_op jit(solution)/shard_map/reduce_scatter | solution.py:144
  558.4 1.9 add_convert_fusion
  (74 shorter events, 11.5 us)
Async XLA Ops:
  6.5 7.7 %copy-start = (bf16[160,1280]{1,0:T(8,128)(2,1)S(1)}, bf16[160,1280]{1,0:T(8,128)(2,1)}, u32[]{:S(2)}) copy-start(bf16[160,1280]{1,0:T(8,128)(2,1)} %param.18) | copy-start | bytes 1228804
  6.5 3.9 copy-start.2
  6.5 3.9 copy-start.10
  6.5 3.9 copy-start.12
  10.5 1.3 copy-start.8
  15.9 43.9 %all-to-all-start = ((bf16[8,64,1280]{2,1,0:T(8,128)(2,1)}), bf16[8,64,1280]{2,1,0:T(8,128)(2,1)S(1)}, u32[]{:S(2)}, u32[]{:S(2)}) async-start(bf16[8,64,1280]{2,1,0:T(8,128)(2,1)} %bitcast.15), calls=%async_computation | async-start | bytes 2621440 | tf_op jit(solution)/shard_map/all_to_all | solution.py:19
  60.0 4.8 copy-start.3
  60.0 5.0 copy-start.9
  60.0 5.0 copy-start.7
  61.2 38.3 %all-to-all-start.1 = ((bf16[8,64,1280]{2,1,0:T(8,128)(2,1)}), bf16[8,64,1280]{2,1,0:T(8,128)(2,1)S(1)}, u32[]{:S(2)}, u32[]{:S(2)}) async-start(bf16[8,64,1280]{2,1,0:T(8,128)(2,1)} %broadcast_in_dim.103), calls=%async_computation.1 | async-start | bytes 2621440 | tf_op jit(solution)/shard_map/all_to_all | solution.py:25
  113.6 8.9 %copy-start.4 = (bf16[112,1184]{1,0:T(8,128)(2,1)S(1)}, bf16[112,1184]{1,0:T(8,128)(2,1)}, u32[]{:S(2)}) copy-start(bf16[112,1184]{1,0:T(8,128)(2,1)} %param.25) | copy-start | bytes 795652
  113.6 8.9 %copy-start.5 = (bf16[112,1184]{1,0:T(8,128)(2,1)S(1)}, bf16[112,1184]{1,0:T(8,128)(2,1)}, u32[]{:S(2)}) copy-start(bf16[112,1184]{1,0:T(8,128)(2,1)} %param.26) | copy-start | bytes 795652
  113.6 8.9 %copy-start.6 = (bf16[1184,112]{0,1:T(8,128)(2,1)S(1)}, bf16[1184,112]{0,1:T(8,128)(2,1)}, u32[]{:S(2)}) copy-start(bf16[1184,112]{0,1:T(8,128)(2,1)} %param.27) | copy-start | bytes 795652
  114.9 24.8 %all-to-all-start.2 = ((bf16[32,32,448]{2,1,0:T(8,128)(2,1)}), bf16[32,32,448]{2,1,0:T(8,128)(2,1)S(1)}, u32[]{:S(2)}, u32[]{:S(2)}) async-start(bf16[32,32,448]{2,1,0:T(8,128)(2,1)} %select_select_fusion), calls=%async_computation.2 | async-start | bytes 2097152 | tf_op jit(solution)/shard_map/all_to_all | solution.py:122
  148.2 316.0 %all-to-all-start.3 = ((bf16[32,112,3552]{2,1,0:T(8,128)(2,1)}), bf16[32,112,3552]{2,1,0:T(8,128)(2,1)}, u32[]{:S(2)}, u32[]{:S(2)}) async-start(bf16[32,112,3552]{2,1,0:T(8,128)(2,1)} %stack.2), calls=%async_computation.3 | async-start | bytes 51380224 | tf_op jit(solution)/shard_map/all_to_all | solution.py:45
  153.6 50.4 %all-gather.2.cloned.1.call-start = ((), (), s32[]{:S(2)}) async-start(), calls=%async_computation.5 | async-start | bytes 4128768 | tf_op jit(solution)/shard_map/all_gather | solution.py:135
  156.9 307.3 %copy-start.11 = (f32[3584]{0:T(1024)S(1)}, f32[3584]{0:T(1024)}, u32[]{:S(2)}) copy-start(f32[3584]{0:T(1024)} %param.24) | copy-start | bytes 43012
  157.9 400.6 %reduce-scatter.2.cloned.1.call-start = ((), (), s32[]{:S(2)}) async-start(), calls=%async_computation.6 | async-start | bytes 4128768 | tf_op jit(solution)/shard_map/reduce_scatter | solution.py:144
  498.8 61.5 %copy-start.1 = (bf16[160,1280]{1,0:T(8,128)(2,1)S(1)}, bf16[160,1280]{1,0:T(8,128)(2,1)}, u32[]{:S(2)}) copy-start(bf16[160,1280]{1,0:T(8,128)(2,1)} %param.18) | copy-start | bytes 1228804
Sparse Core Ops, SparseCore 0:
  158.0 45.9 all-gather.1
  498.9 59.4 reduce-scatter.1
